TPU v7x, 32 devices: a whole 2x2x4 slice. The times are simulated.
32 devices in a mesh: gx: 4 (over y, x), gy: 8 (over z, core).
Axes of the slice: x: 2, y: 2, z: 4, core: 2. Of those that a mesh axis runs over, the one named last changes fastest.
Arguments:
- features: bfloat16 [64, 512, 128], P(('gx', 'gy')), may hold values from -11 to 11
- brick_pos: int32 [64], P(('gx', 'gy')), may hold values from 0 to 4, as said below
- cotangent: bfloat16 [64, 512, 128], P(('gx', 'gy')), may hold values from -40 to 40
- first_kernel: bfloat16 [27, 128, 128], replicated, may hold values from -0.109375 to 0.109375
- second_kernel: bfloat16 [27, 128, 128], replicated, may hold values from -0.109375 to 0.109375
- norm_gain: float32 [128], replicated, may hold values from 0.1 to 1.9
Outputs:
- block_out: bfloat16 [64, 512, 128], P(('gx', 'gy'))
- feature_grad: bfloat16 [64, 512, 128], P(('gx', 'gy'))
- kernel_update: float32 [2, 27, 128, 128], replicated
- gain_update: float32 [128], replicated
Inputs may be any that keep to these rules, and one draw needn't show every extreme that they name: `brick_pos`: on each device block the first k slots (k between max(1, 0) and 2, and k = 2 on at least one block) hold distinct positions below 4; the remaining slots hold 4.
All inputs are finite; a program needn't handle non-finite values.
Results may differ from a plain program's by a relative error of at most 0.0029.
Values may be sent and summed in bfloat16 or wider, within the bound.
No kernel may reach another device: no remote copies, remote signals or barrier semaphores. Data moves between devices by JAX's collectives and lax.ppermute only.
A program may use at most 128 MiB of HBM per device.

v0:
```python
import jax
import jax.numpy as jnp
from jax import lax
from jax.sharding import PartitionSpec as P

BX = 2
BY = 2
BZ = 1
POS = 4
clip_level = 0.5


def with_halo(cells, sides, width):
    for axis, dim in sides:
        count = lax.axis_size(axis)
        ends = count - 1
        head = lax.slice_in_dim(cells, 0, width, axis=dim)
        tail = lax.slice_in_dim(cells, cells.shape[dim] - width, cells.shape[dim], axis=dim)
        cells = jnp.concatenate(
            [
                lax.ppermute(tail, axis, [(i, (i + 1) % count) for i in range(ends)]),
                cells,
                lax.ppermute(head, axis, [((i + 1) % count, i) for i in range(ends)]),
            ],
            axis=dim,
        )
    return cells


def brick_coords(position):
    brick_x = position // (BY * BZ)
    brick_y = position // BZ % BY
    brick_z = position % BZ
    return (brick_x, brick_y, brick_z)


def activate(pre, norm_gain):
    average = jnp.mean(pre, axis=-1, keepdims=True)
    center = pre - average
    spread = jnp.mean(center * center, axis=-1, keepdims=True)
    normed = center * lax.rsqrt(spread + 1e-05) * norm_gain
    return normed * jax.nn.sigmoid(normed)


def apply_taps(tile_set, kernel, flipped):
    slot_count, channels = (tile_set.shape[0], tile_set.shape[-1])
    summed = jnp.zeros((slot_count * 512, channels), jnp.float32)
    for step_x in range(3):
        for step_y in range(3):
            for step_z in range(3):
                tap_index = (step_x * 3 + step_y) * 3 + step_z
                if flipped:
                    start_x, start_y, start_z = (2 - step_x, 2 - step_y, 2 - step_z)
                else:
                    start_x, start_y, start_z = (step_x, step_y, step_z)
                window = tile_set[
                    :, start_x : start_x + 8, start_y : start_y + 8, start_z : start_z + 8, :
                ]
                window = window.reshape(slot_count * 512, channels)
                if flipped:
                    summed = summed + lax.dot_general(
                        window,
                        kernel[tap_index],
                        (((1,), (1,)), ((), ())),
                        preferred_element_type=jnp.float32,
                    )
                else:
                    summed = summed + jnp.dot(
                        window, kernel[tap_index], preferred_element_type=jnp.float32
                    )
    return summed.reshape(slot_count, 512, channels)


def tap_grads(tile_set, upstream):
    slot_count, channels = (tile_set.shape[0], tile_set.shape[-1])
    flat_rows = upstream.reshape(slot_count * 512, channels)
    result = []
    for step_x in range(3):
        for step_y in range(3):
            for step_z in range(3):
                window = tile_set[
                    :, step_x : step_x + 8, step_y : step_y + 8, step_z : step_z + 8, :
                ]
                window = window.reshape(slot_count * 512, channels)
                result.append(
                    lax.dot_general(
                        window,
                        flat_rows,
                        (((0,), (0,)), ((), ())),
                        preferred_element_type=jnp.float32,
                    )
                )
    return jnp.stack(result)


def widen_grid(dense_grid):
    widened = with_halo(dense_grid, (("gx", 0), ("gy", 1)), 1)
    return jnp.pad(widened, ((0, 0), (0, 0), (1, 1), (0, 0)))


def clip_factor(squares, channels):
    entries = 54.0 * channels * channels + channels
    return jnp.minimum(1.0, clip_level / jnp.sqrt(squares / entries + 1e-06))


def per_device(features, brick_pos, cotangent, first_kernel, second_kernel, norm_gain):
    slot_count, channels = (features.shape[0], features.shape[2])
    is_live = brick_pos < POS
    brick_x, brick_y, brick_z = brick_coords(jnp.minimum(brick_pos, POS - 1))
    put_x = jnp.where(is_live, brick_x, BX)
    live_mask = is_live[:, None, None]
    given_rows = jnp.where(live_mask, features, jnp.zeros_like(features))
    upstream = jnp.where(live_mask, cotangent, jnp.zeros_like(cotangent))

    def tiles_for(values):
        bricks = jnp.zeros((BX, BY, BZ, 8, 8, 8, channels), values.dtype)
        bricks = bricks.at[put_x, brick_y, brick_z].set(
            values.reshape(slot_count, 8, 8, 8, channels), mode="drop"
        )
        dense_grid = bricks.transpose(0, 3, 1, 4, 2, 5, 6).reshape(BX * 8, BY * 8, BZ * 8, channels)
        padded = widen_grid(dense_grid)

        def take_tile(start_x, start_y, start_z):
            return lax.dynamic_slice(
                padded, (start_x * 8, start_y * 8, start_z * 8, start_x * 0), (10, 10, 10, channels)
            )

        return jax.vmap(take_tile)(brick_x, brick_y, brick_z)

    given_tiles = tiles_for(given_rows)
    first_pre = jnp.where(live_mask, apply_taps(given_tiles, first_kernel, False), 0.0)
    hidden_full, pullback = jax.vjp(activate, first_pre, norm_gain)
    hidden = jnp.where(live_mask, hidden_full, 0.0).astype(jnp.bfloat16)
    hidden_tiles = tiles_for(hidden)
    second_pre = jnp.where(live_mask, apply_taps(hidden_tiles, second_kernel, False), 0.0)
    block_out = (given_rows.astype(jnp.float32) + second_pre).astype(jnp.bfloat16)
    second_grad = tap_grads(hidden_tiles, upstream).reshape(-1)
    hidden_grad = jnp.where(live_mask, apply_taps(tiles_for(upstream), second_kernel, True), 0.0)
    pre_full, gain_grad = pullback(hidden_grad)
    pre_grad = jnp.where(live_mask, pre_full, 0.0).astype(jnp.bfloat16)
    first_grad = tap_grads(given_tiles, pre_grad).reshape(-1)
    back_conv = apply_taps(tiles_for(pre_grad), first_kernel, True)
    feature_grad = jnp.where(live_mask, upstream.astype(jnp.float32) + back_conv, 0.0).astype(
        jnp.bfloat16
    )
    combined, gain_summed = lax.psum(
        (jnp.concatenate([first_grad, second_grad]), gain_grad), ("gx", "gy")
    )
    shrink = clip_factor(
        jnp.sum(combined * combined) + jnp.sum(gain_summed * gain_summed), channels
    )
    updated = shrink * combined
    kernel_update = updated.reshape(2, 27, channels, channels)
    return (block_out, feature_grad, kernel_update, shrink * gain_summed)


def solution(mesh):
    in_specs = (
        P(("gx", "gy"), None, None),
        P(("gx", "gy")),
        P(("gx", "gy"), None, None),
        P(),
        P(),
        P(),
    )
    out_specs = (P(("gx", "gy"), None, None), P(("gx", "gy"), None, None), P(), P())
    return jax.shard_map(
        per_device, mesh=mesh, in_specs=in_specs, out_specs=out_specs, check_vma=False
    )
```

profile of v0, /device:TPU:0, one launch (start us, length us, event | category | flops | bytes accessed | tf_op | source)
XLA Modules:
  0.0 331.9 jit_solution(15290965411382618557)
XLA Ops:
  7.2 0.7 fusion.288
  9.2 1.1 broadcast_select_fusion
  10.5 0.7 scatter_fusion.2
  11.2 4.9 %collective-permute-start.8 = (bf16[1,16,8,128]{3,2,1,0:T(8,128)(2,1)S(1)}, bf16[1,16,8,128]{3,2,1,0:T(8,128)(2,1)S(1)}, u32[]{:S(2)}, u32[]{:S(2)}) collective-permute-start(bf16[1,16,8,128]{3,2,1,0:T(8,128)(2,1)S(1)} %get-tuple-element.24), channel_id=1, source_target_pairs={{0,8},{8,16},{16,24},{1,9},{9,17},{17,25},{2,10},{10,18},{18,26},{... | collective-permute-start | bytes 98312 | tf_op jit(solution)/shard_map/ppermute | solution.py:21
  16.1 1.3 collective-permute-start.9
  18.3 4.5 %collective-permute-start = (bf16[1,16,8,128]{3,2,1,0:T(8,128)(2,1)S(1)}, bf16[1,16,8,128]{3,2,1,0:T(8,128)(2,1)S(1)}, u32[]{:S(2)}, u32[]{:S(2)}) collective-permute-start(bf16[1,16,8,128]{3,2,1,0:T(8,128)(2,1)S(1)} %get-tuple-element.28), channel_id=1, source_target_pairs={{0,8},{8,16},{16,24},{1,9},{9,17},{17,25},{2,10},{10,18},{18,26},{... | collective-permute-start | bytes 98312 | tf_op jit(solution)/shard_map/ppermute | solution.py:21
  22.8 1.3 collective-permute-start.1
  24.2 1.3 collective-permute-start.10
  25.5 1.3 collective-permute-start.11
  26.9 2.1 collective-permute-done.1
  29.0 2.7 collective-permute-start.2
  31.7 1.3 collective-permute-start.3
  33.8 2.7 pad_slice_fusion.18
  36.6 1.4 fusion.300
  39.2 1.1 pad_slice_fusion.54
  56.1 2.5 multiply_reduce_fusion.1
  58.8 2.7 fusion.293
  61.6 1.5 select_convert_fusion
  63.3 1.3 fusion.52
  71.9 1.2 copy-done.96
  73.3 2.3 fusion.62
  76.5 4.9 %collective-permute-start.4 = (bf16[1,16,8,128]{3,2,1,0:T(8,128)(2,1)S(1)}, bf16[1,16,8,128]{3,2,1,0:T(8,128)(2,1)S(1)}, u32[]{:S(2)}, u32[]{:S(2)}) collective-permute-start(bf16[1,16,8,128]{3,2,1,0:T(8,128)(2,1)S(1)} %get-tuple-element.26), channel_id=1, source_target_pairs={{0,8},{8,16},{16,24},{1,9},{9,17},{17,25},{2,10},{10,18},{18,26},{... | collective-permute-start | bytes 98312 | tf_op jit(solution)/shard_map/ppermute | solution.py:21
  81.4 1.3 collective-permute-start.5
  82.7 45.0 %psum.15 = f32[128]{0:T(128)S(1)} all-reduce(f32[128]{0:T(128)S(1)} %copy-done.163), channel_id=1, replica_groups=mesh['gx'=4,'gy'=8] {'gx','gy'}, use_global_device_ids=true, to_apply=%region_11.12 | all-reduce | flops 128 | bytes 1024 | tf_op jit(solution)/shard_map/psum | solution.py:146
  128.5 0.8 copy-done.2
  129.3 1.1 copy.13
  131.0 4.2 %collective-permute-start.12 = (bf16[1,16,8,128]{3,2,1,0:T(8,128)(2,1)S(1)}, bf16[1,16,8,128]{3,2,1,0:T(8,128)(2,1)S(1)}, u32[]{:S(2)}, u32[]{:S(2)}) collective-permute-start(bf16[1,16,8,128]{3,2,1,0:T(8,128)(2,1)S(1)} %get-tuple-element.22), channel_id=1, source_target_pairs={{0,8},{8,16},{16,24},{1,9},{9,17},{17,25},{2,10},{10,18},{18,26},{... | collective-permute-start | bytes 98312 | tf_op jit(solution)/shard_map/ppermute | solution.py:21
  135.2 1.3 collective-permute-start.13
  136.6 1.3 collective-permute-start.6
  137.9 1.3 collective-permute-start.7
  139.2 1.8 collective-permute-done.13
  141.7 3.5 %collective-permute-start.14 = (bf16[18,1,8,128]{3,2,1,0:T(8,128)(2,1)}, bf16[18,1,8,128]{3,2,1,0:T(8,128)(2,1)}, u32[]{:S(2)}, u32[]{:S(2)}) collective-permute-start(bf16[18,1,8,128]{3,2,1,0:T(8,128)(2,1)} %get-tuple-element.14), channel_id=1, source_target_pairs={{0,1},{1,2},{2,3},{3,4},{4,5},{5,6},{6,7},{8,9},{9,10},{10,11},{11... | collective-permute-start | bytes 110600 | tf_op jit(solution)/shard_map/ppermute | solution.py:21
  145.2 1.5 collective-permute-start.15
  146.7 1.0 pad_maximum_fusion.2
  147.7 1.8 gather_fusion.1
  149.5 2.7 pad_slice_fusion.36
  152.3 1.3 fusion.301
  153.6 1.8 pad_maximum_fusion.4
  155.3 1.8 gather_fusion.3
  157.2 2.7 pad_slice_fusion
  159.9 1.4 fusion.299
  161.3 1.0 fusion.117
  170.3 2.0 pad_maximum_fusion
  172.3 1.4 convolution_add_fusion.77
  190.8 1.0 select_convert_fusion.1
  191.8 123.8 %all-reduce.6.cloned.1.call-done = f32[884736]{0:T(1024)} async-done(((f32[884736]{0:T(1024)}), f32[884736]{0:T(1024)}) %all-reduce.6.cloned.1.call-update) | async-done | bytes 3538960 | tf_op jit(solution)/shard_map/psum | solution.py:146
  315.6 3.5 %multiply_reduce_fusion = f32[]{:T(128)} fusion(f32[884736]{0:T(1024)} %all-reduce.6.cloned.1.call-done), kind=kLoop, calls=%fused_computation.9 | loop fusion | flops 1769471 | bytes 3538948 | tf_op jit(solution)/shard_map/reduce_sum | solution.py:150
  321.0 4.0 %broadcast_multiply_fusion = f32[884736]{0:T(1024)} fusion(f32[884736]{0:T(1024)} %all-reduce.6.cloned.1.call-done, f32[]{:T(128)S(6)} %min.7), kind=kLoop, calls=%fused_computation.82 | loop fusion | flops 884736 | bytes 7077892 | tf_op jit(solution)/shard_map/mul | solution.py:152
  (539 shorter events, 54.2 us)
Async XLA Ops:
  7.2 308.5 %all-reduce.6.cloned.1.call-start = ((), (), s32[]{:S(2)}) async-start(), calls=%async_computation | async-start | bytes 7077888 | tf_op jit(solution)/shard_map/psum | solution.py:146
  7.9 30.2 %copy-start.155 = (s32[2]{0:T(128)}, s32[2]{0:T(128)S(1)}, u32[]{:S(2)}) copy-start(s32[2]{0:T(128)S(1)} %get-tuple-element.9) | copy-start | bytes 28
  8.6 15.5 %copy-start.156 = (pred[2]{0:T(512)(128)(4,1)}, pred[2]{0:T(512)(128)(4,1)S(1)}, u32[]{:S(2)}) copy-start(pred[2]{0:T(512)(128)(4,1)S(1)} %broadcast_compare_fusion) | copy-start | bytes 10
  11.2 13.0 %collective-permute-start.8 = (bf16[1,16,8,128]{3,2,1,0:T(8,128)(2,1)S(1)}, bf16[1,16,8,128]{3,2,1,0:T(8,128)(2,1)S(1)}, u32[]{:S(2)}, u32[]{:S(2)}) collective-permute-start(bf16[1,16,8,128]{3,2,1,0:T(8,128)(2,1)S(1)} %get-tuple-element.24), channel_id=1, source_target_pairs={{0,8},{8,16},{16,24},{1,9},{9,17},{17,25},{2,10},{10,18},{18,26},{... | collective-permute-start | bytes 98312 | tf_op jit(solution)/shard_map/ppermute | solution.py:21
  16.1 8.1 %collective-permute-start.9 = (bf16[1,16,8,128]{3,2,1,0:T(8,128)(2,1)S(1)}, bf16[1,16,8,128]{3,2,1,0:T(8,128)(2,1)S(1)}, u32[]{:S(2)}, u32[]{:S(2)}) collective-permute-start(bf16[1,16,8,128]{3,2,1,0:T(8,128)(2,1)S(1)} %get-tuple-element.25), channel_id=1, source_target_pairs={{8,0},{16,8},{24,16},{9,1},{17,9},{25,17},{10,2},{18,10},{26,18},{... | collective-permute-start | bytes 98312 | tf_op jit(solution)/shard_map/ppermute | solution.py:23
  18.3 8.6 %collective-permute-start = (bf16[1,16,8,128]{3,2,1,0:T(8,128)(2,1)S(1)}, bf16[1,16,8,128]{3,2,1,0:T(8,128)(2,1)S(1)}, u32[]{:S(2)}, u32[]{:S(2)}) collective-permute-start(bf16[1,16,8,128]{3,2,1,0:T(8,128)(2,1)S(1)} %get-tuple-element.28), channel_id=1, source_target_pairs={{0,8},{8,16},{16,24},{1,9},{9,17},{17,25},{2,10},{10,18},{18,26},{... | collective-permute-start | bytes 98312 | tf_op jit(solution)/shard_map/ppermute | solution.py:21
  22.8 6.2 %collective-permute-start.1 = (bf16[1,16,8,128]{3,2,1,0:T(8,128)(2,1)S(1)}, bf16[1,16,8,128]{3,2,1,0:T(8,128)(2,1)S(1)}, u32[]{:S(2)}, u32[]{:S(2)}) collective-permute-start(bf16[1,16,8,128]{3,2,1,0:T(8,128)(2,1)S(1)} %get-tuple-element.29), channel_id=1, source_target_pairs={{8,0},{16,8},{24,16},{9,1},{17,9},{25,17},{10,2},{18,10},{26,18},{... | collective-permute-start | bytes 98312 | tf_op jit(solution)/shard_map/ppermute | solution.py:23
  24.2 8.8 %collective-permute-start.10 = (bf16[18,1,8,128]{3,2,1,0:T(8,128)(2,1)S(1)}, bf16[18,1,8,128]{3,2,1,0:T(8,128)(2,1)S(1)}, u32[]{:S(2)}, u32[]{:S(2)}) collective-permute-start(bf16[18,1,8,128]{3,2,1,0:T(8,128)(2,1)S(1)} %get-tuple-element.16), channel_id=1, source_target_pairs={{0,1},{1,2},{2,3},{3,4},{4,5},{5,6},{6,7},{8,9},{9,10},{10,11},{11... | collective-permute-start | bytes 110600 | tf_op jit(solution)/shard_map/ppermute | solution.py:21
  25.5 7.5 %collective-permute-start.11 = (bf16[18,1,8,128]{3,2,1,0:T(8,128)(2,1)S(1)}, bf16[18,1,8,128]{3,2,1,0:T(8,128)(2,1)S(1)}, u32[]{:S(2)}, u32[]{:S(2)}) collective-permute-start(bf16[18,1,8,128]{3,2,1,0:T(8,128)(2,1)S(1)} %get-tuple-element.17), channel_id=1, source_target_pairs={{1,0},{2,1},{3,2},{4,3},{5,4},{6,5},{7,6},{9,8},{10,9},{11,10},{12... | collective-permute-start | bytes 110600 | tf_op jit(solution)/shard_map/ppermute | solution.py:23
  29.0 8.9 %collective-permute-start.2 = (bf16[18,1,8,128]{3,2,1,0:T(8,128)(2,1)S(1)}, bf16[18,1,8,128]{3,2,1,0:T(8,128)(2,1)S(1)}, u32[]{:S(2)}, u32[]{:S(2)}) collective-permute-start(bf16[18,1,8,128]{3,2,1,0:T(8,128)(2,1)S(1)} %get-tuple-element.20), channel_id=1, source_target_pairs={{0,1},{1,2},{2,3},{3,4},{4,5},{5,6},{6,7},{8,9},{9,10},{10,11},{11... | collective-permute-start | bytes 110600 | tf_op jit(solution)/shard_map/ppermute | solution.py:21
  31.7 6.2 %collective-permute-start.3 = (bf16[18,1,8,128]{3,2,1,0:T(8,128)(2,1)S(1)}, bf16[18,1,8,128]{3,2,1,0:T(8,128)(2,1)S(1)}, u32[]{:S(2)}, u32[]{:S(2)}) collective-permute-start(bf16[18,1,8,128]{3,2,1,0:T(8,128)(2,1)S(1)} %get-tuple-element.21), channel_id=1, source_target_pairs={{1,0},{2,1},{3,2},{4,3},{5,4},{6,5},{7,6},{9,8},{10,9},{11,10},{12... | collective-permute-start | bytes 110600 | tf_op jit(solution)/shard_map/ppermute | solution.py:23
  39.1 3.3 copy-start.31
  39.1 4.0 %copy-start.25 = (bf16[2,8,8,8,128]{4,3,2,1,0:T(8,128)(2,1)}, bf16[2,8,8,8,128]{4,3,2,1,0:T(8,128)(2,1)S(1)}, u32[]{:S(2)}) copy-start(bf16[2,8,8,8,128]{4,3,2,1,0:T(8,128)(2,1)S(1)} %get-tuple-element.133) | copy-start | bytes 786436
  39.1 4.6 %copy-start.17 = (bf16[2,8,8,8,128]{4,3,2,1,0:T(8,128)(2,1)}, bf16[2,8,8,8,128]{4,3,2,1,0:T(8,128)(2,1)S(1)}, u32[]{:S(2)}) copy-start(bf16[2,8,8,8,128]{4,3,2,1,0:T(8,128)(2,1)S(1)} %get-tuple-element.132) | copy-start | bytes 786436
  39.1 5.3 %copy-start.7 = (bf16[2,8,8,8,128]{4,3,2,1,0:T(8,128)(2,1)}, bf16[2,8,8,8,128]{4,3,2,1,0:T(8,128)(2,1)S(1)}, u32[]{:S(2)}) copy-start(bf16[2,8,8,8,128]{4,3,2,1,0:T(8,128)(2,1)S(1)} %get-tuple-element.131) | copy-start | bytes 786436
  40.3 3.0 copy-start.33
  40.3 3.2 copy-start.29
  40.3 3.7 %copy-start.27 = (bf16[2,8,8,8,128]{4,3,2,1,0:T(8,128)(2,1)}, bf16[2,8,8,8,128]{4,3,2,1,0:T(8,128)(2,1)S(1)}, u32[]{:S(2)}) copy-start(bf16[2,8,8,8,128]{4,3,2,1,0:T(8,128)(2,1)S(1)} %get-tuple-element.120) | copy-start | bytes 786436
  40.3 3.9 %copy-start.23 = (bf16[2,8,8,8,128]{4,3,2,1,0:T(8,128)(2,1)}, bf16[2,8,8,8,128]{4,3,2,1,0:T(8,128)(2,1)S(1)}, u32[]{:S(2)}) copy-start(bf16[2,8,8,8,128]{4,3,2,1,0:T(8,128)(2,1)S(1)} %get-tuple-element.121) | copy-start | bytes 786436
  40.3 4.3 %copy-start.21 = (bf16[2,8,8,8,128]{4,3,2,1,0:T(8,128)(2,1)}, bf16[2,8,8,8,128]{4,3,2,1,0:T(8,128)(2,1)S(1)}, u32[]{:S(2)}) copy-start(bf16[2,8,8,8,128]{4,3,2,1,0:T(8,128)(2,1)S(1)} %get-tuple-element.122) | copy-start | bytes 786436
  40.3 4.6 %copy-start.19 = (bf16[2,8,8,8,128]{4,3,2,1,0:T(8,128)(2,1)}, bf16[2,8,8,8,128]{4,3,2,1,0:T(8,128)(2,1)S(1)}, u32[]{:S(2)}) copy-start(bf16[2,8,8,8,128]{4,3,2,1,0:T(8,128)(2,1)S(1)} %get-tuple-element.123) | copy-start | bytes 786436
  40.3 4.8 %copy-start.15 = (bf16[2,8,8,8,128]{4,3,2,1,0:T(8,128)(2,1)}, bf16[2,8,8,8,128]{4,3,2,1,0:T(8,128)(2,1)S(1)}, u32[]{:S(2)}) copy-start(bf16[2,8,8,8,128]{4,3,2,1,0:T(8,128)(2,1)S(1)} %get-tuple-element.129) | copy-start | bytes 786436
  40.4 5.0 %copy-start.13 = (bf16[2,8,8,8,128]{4,3,2,1,0:T(8,128)(2,1)}, bf16[2,8,8,8,128]{4,3,2,1,0:T(8,128)(2,1)S(1)}, u32[]{:S(2)}) copy-start(bf16[2,8,8,8,128]{4,3,2,1,0:T(8,128)(2,1)S(1)} %get-tuple-element.124) | copy-start | bytes 786436
  40.4 5.2 %copy-start.11 = (bf16[2,8,8,8,128]{4,3,2,1,0:T(8,128)(2,1)}, bf16[2,8,8,8,128]{4,3,2,1,0:T(8,128)(2,1)S(1)}, u32[]{:S(2)}) copy-start(bf16[2,8,8,8,128]{4,3,2,1,0:T(8,128)(2,1)S(1)} %get-tuple-element.125) | copy-start | bytes 786436
  40.4 5.4 %copy-start.9 = (bf16[2,8,8,8,128]{4,3,2,1,0:T(8,128)(2,1)}, bf16[2,8,8,8,128]{4,3,2,1,0:T(8,128)(2,1)S(1)}, u32[]{:S(2)}) copy-start(bf16[2,8,8,8,128]{4,3,2,1,0:T(8,128)(2,1)S(1)} %get-tuple-element.128) | copy-start | bytes 786436
  40.4 5.6 %copy-start.5 = (bf16[2,8,8,8,128]{4,3,2,1,0:T(8,128)(2,1)}, bf16[2,8,8,8,128]{4,3,2,1,0:T(8,128)(2,1)S(1)}, u32[]{:S(2)}) copy-start(bf16[2,8,8,8,128]{4,3,2,1,0:T(8,128)(2,1)S(1)} %get-tuple-element.126) | copy-start | bytes 786436
  40.4 5.9 %copy-start.3 = (bf16[2,8,8,8,128]{4,3,2,1,0:T(8,128)(2,1)}, bf16[2,8,8,8,128]{4,3,2,1,0:T(8,128)(2,1)S(1)}, u32[]{:S(2)}) copy-start(bf16[2,8,8,8,128]{4,3,2,1,0:T(8,128)(2,1)S(1)} %get-tuple-element.127) | copy-start | bytes 786436
  61.5 3.1 copy-start.51
  61.5 3.4 %copy-start.48 = (bf16[2,8,8,8,128]{4,3,2,1,0:T(8,128)(2,1)S(1)}, bf16[2,8,8,8,128]{4,3,2,1,0:T(8,128)(2,1)}, u32[]{:S(2)}) copy-start(bf16[2,8,8,8,128]{4,3,2,1,0:T(8,128)(2,1)} %copy-done.47) | copy-start | bytes 786436
  61.5 3.7 %copy-start.40 = (bf16[2,8,8,8,128]{4,3,2,1,0:T(8,128)(2,1)S(1)}, bf16[2,8,8,8,128]{4,3,2,1,0:T(8,128)(2,1)}, u32[]{:S(2)}) copy-start(bf16[2,8,8,8,128]{4,3,2,1,0:T(8,128)(2,1)} %copy-done.39) | copy-start | bytes 786436
  61.5 3.9 %copy-start.44 = (bf16[2,8,8,8,128]{4,3,2,1,0:T(8,128)(2,1)S(1)}, bf16[2,8,8,8,128]{4,3,2,1,0:T(8,128)(2,1)}, u32[]{:S(2)}) copy-start(bf16[2,8,8,8,128]{4,3,2,1,0:T(8,128)(2,1)} %copy-done.43) | copy-start | bytes 786436
  63.0 2.8 copy-start.42
  63.3 2.8 copy-start.32
  70.5 2.8 copy-start.157
  70.5 2.8 copy-start.160
  73.3 9.4 %copy-start.163 = (f32[128]{0:T(128)S(1)}, f32[128]{0:T(128)}, u32[]{:S(2)}) copy-start(f32[128]{0:T(128)} %get-tuple-element.4) | copy-start | bytes 1540
  75.6 52.2 %copy-start.100 = (bf16[2,8,8,8,128]{4,3,2,1,0:T(8,128)(2,1)S(1)}, bf16[2,8,8,8,128]{4,3,2,1,0:T(8,128)(2,1)}, u32[]{:S(2)}) copy-start(bf16[2,8,8,8,128]{4,3,2,1,0:T(8,128)(2,1)} %get-tuple-element.12) | copy-start | bytes 786436
  76.5 60.1 %collective-permute-start.4 = (bf16[1,16,8,128]{3,2,1,0:T(8,128)(2,1)S(1)}, bf16[1,16,8,128]{3,2,1,0:T(8,128)(2,1)S(1)}, u32[]{:S(2)}, u32[]{:S(2)}) collective-permute-start(bf16[1,16,8,128]{3,2,1,0:T(8,128)(2,1)S(1)} %get-tuple-element.26), channel_id=1, source_target_pairs={{0,8},{8,16},{16,24},{1,9},{9,17},{17,25},{2,10},{10,18},{18,26},{... | collective-permute-start | bytes 98312 | tf_op jit(solution)/shard_map/ppermute | solution.py:21
  81.4 55.2 %collective-permute-start.5 = (bf16[1,16,8,128]{3,2,1,0:T(8,128)(2,1)S(1)}, bf16[1,16,8,128]{3,2,1,0:T(8,128)(2,1)S(1)}, u32[]{:S(2)}, u32[]{:S(2)}) collective-permute-start(bf16[1,16,8,128]{3,2,1,0:T(8,128)(2,1)S(1)} %get-tuple-element.27), channel_id=1, source_target_pairs={{8,0},{16,8},{24,16},{9,1},{17,9},{25,17},{10,2},{18,10},{26,18},{... | collective-permute-start | bytes 98312 | tf_op jit(solution)/shard_map/ppermute | solution.py:23
  127.7 8.9 %copy-start.161 = (f32[128]{0:T(128)}, f32[128]{0:T(128)S(1)}, u32[]{:S(2)}) copy-start(f32[128]{0:T(128)S(1)} %psum.15) | copy-start | bytes 1540
  131.0 8.1 %collective-permute-start.12 = (bf16[1,16,8,128]{3,2,1,0:T(8,128)(2,1)S(1)}, bf16[1,16,8,128]{3,2,1,0:T(8,128)(2,1)S(1)}, u32[]{:S(2)}, u32[]{:S(2)}) collective-permute-start(bf16[1,16,8,128]{3,2,1,0:T(8,128)(2,1)S(1)} %get-tuple-element.22), channel_id=1, source_target_pairs={{0,8},{8,16},{16,24},{1,9},{9,17},{17,25},{2,10},{10,18},{18,26},{... | collective-permute-start | bytes 98312 | tf_op jit(solution)/shard_map/ppermute | solution.py:21
  135.2 5.8 %collective-permute-start.13 = (bf16[1,16,8,128]{3,2,1,0:T(8,128)(2,1)S(1)}, bf16[1,16,8,128]{3,2,1,0:T(8,128)(2,1)S(1)}, u32[]{:S(2)}, u32[]{:S(2)}) collective-permute-start(bf16[1,16,8,128]{3,2,1,0:T(8,128)(2,1)S(1)} %get-tuple-element.23), channel_id=1, source_target_pairs={{8,0},{16,8},{24,16},{9,1},{17,9},{25,17},{10,2},{18,10},{26,18},{... | collective-permute-start | bytes 98312 | tf_op jit(solution)/shard_map/ppermute | solution.py:23
  136.6 10.1 %collective-permute-start.6 = (bf16[18,1,8,128]{3,2,1,0:T(8,128)(2,1)S(1)}, bf16[18,1,8,128]{3,2,1,0:T(8,128)(2,1)S(1)}, u32[]{:S(2)}, u32[]{:S(2)}) collective-permute-start(bf16[18,1,8,128]{3,2,1,0:T(8,128)(2,1)S(1)} %get-tuple-element.18), channel_id=1, source_target_pairs={{0,1},{1,2},{2,3},{3,4},{4,5},{5,6},{6,7},{8,9},{9,10},{10,11},{11... | collective-permute-start | bytes 110600 | tf_op jit(solution)/shard_map/ppermute | solution.py:21
  137.9 8.8 %collective-permute-start.7 = (bf16[18,1,8,128]{3,2,1,0:T(8,128)(2,1)S(1)}, bf16[18,1,8,128]{3,2,1,0:T(8,128)(2,1)S(1)}, u32[]{:S(2)}, u32[]{:S(2)}) collective-permute-start(bf16[18,1,8,128]{3,2,1,0:T(8,128)(2,1)S(1)} %get-tuple-element.19), channel_id=1, source_target_pairs={{1,0},{2,1},{3,2},{4,3},{5,4},{6,5},{7,6},{9,8},{10,9},{11,10},{12... | collective-permute-start | bytes 110600 | tf_op jit(solution)/shard_map/ppermute | solution.py:23
  141.7 11.9 %collective-permute-start.14 = (bf16[18,1,8,128]{3,2,1,0:T(8,128)(2,1)}, bf16[18,1,8,128]{3,2,1,0:T(8,128)(2,1)}, u32[]{:S(2)}, u32[]{:S(2)}) collective-permute-start(bf16[18,1,8,128]{3,2,1,0:T(8,128)(2,1)} %get-tuple-element.14), channel_id=1, source_target_pairs={{0,1},{1,2},{2,3},{3,4},{4,5},{5,6},{6,7},{8,9},{9,10},{10,11},{11... | collective-permute-start | bytes 110600 | tf_op jit(solution)/shard_map/ppermute | solution.py:21
  145.2 8.4 %collective-permute-start.15 = (bf16[18,1,8,128]{3,2,1,0:T(8,128)(2,1)}, bf16[18,1,8,128]{3,2,1,0:T(8,128)(2,1)}, u32[]{:S(2)}, u32[]{:S(2)}) collective-permute-start(bf16[18,1,8,128]{3,2,1,0:T(8,128)(2,1)} %get-tuple-element.15), channel_id=1, source_target_pairs={{1,0},{2,1},{3,2},{4,3},{5,4},{6,5},{7,6},{9,8},{10,9},{11,10},{12... | collective-permute-start | bytes 110600 | tf_op jit(solution)/shard_map/ppermute | solution.py:23
  159.9 2.7 copy-start.95
  191.8 128.7 %copy-start.162 = (f32[128]{0:T(128)S(1)}, f32[128]{0:T(128)}, u32[]{:S(2)}) copy-start(f32[128]{0:T(128)} %copy-done.161) | copy-start | bytes 1540
  (133 other events, 178.6 us)
Sparse Core Ops, SparseCore 0:
  172.4 143.1 all-reduce.5
where the time goes:
time: 334 us; the launch traced here: 332 us
  waiting for transfers between devices  128 us (38%)
  blocking collectives  45 us (13%)
  matrix products  43.2 us (13%)
  starting transfers between devices  37.9 us (11%)
  local copies, waits for them, and re-layouts  33.8 us (10%)
  other arithmetic  25.6 us (8%)
  between operations  18.6 us (6%)
    psum x1, waiting for transfers between devices, per_device(): lax.psum((jnp.concatenate([first_grad, second_grad]), gain_grad), ('gx',...  124 us
    psum x1, blocking collectives, per_device(): lax.psum((jnp.concatenate([first_grad, second_grad]), gain_grad), ('gx',...  45 us
    ppermute x8, starting transfers between devices, with_halo(): lax.ppermute(tail, axis, [(i, (i + 1) % count) for i in range(ends)])  27.3 us
    dot_general x54, matrix products, tap_grads(): lax.dot_general(window, flat_rows, (((0,), (0,)), ((), ())), preferred_el...  15.4 us
    dot_general x54, matrix products, apply_taps(): lax.dot_general(window, kernel[tap_index], (((1,), (1,)), ((), ())), pref...  14.3 us
    slice x8, local copies, waits for them, and re-layouts, apply_taps(): tile_set[:, start_x:start_x + 8, start_y:start_y + 8, start_z:start_z + 8...  13.6 us
    dot_general x54, matrix products, apply_taps(): jnp.dot(window, kernel[tap_index], preferred_element_type=jnp.float32)  13.4 us
    ppermute x8, starting transfers between devices, with_halo(): lax.ppermute(head, axis, [((i + 1) % count, i) for i in range(ends)])  10.5 us
  transfers between devices with their start and end apart: 17, of which 3 were waited for; matrix products, arithmetic and copies ran while one was open for 9% of the time, Pallas kernels for 0%

commit v1 on v0

--- a/solution.py
+++ b/solution.py
@@ -8,6 +8,11 @@
 BZ = 1
 POS = 4
 clip_level = 0.5
+
+
+def axis_by_axis(value, inner_axis, outer_axis):
+    inner = lax.psum(value, inner_axis)
+    return lax.psum(inner, outer_axis)
 
 
 def with_halo(cells, sides, width):
@@ -143,8 +148,8 @@
     feature_grad = jnp.where(live_mask, upstream.astype(jnp.float32) + back_conv, 0.0).astype(
         jnp.bfloat16
     )
-    combined, gain_summed = lax.psum(
-        (jnp.concatenate([first_grad, second_grad]), gain_grad), ("gx", "gy")
+    combined, gain_summed = axis_by_axis(
+        (jnp.concatenate([first_grad, second_grad]), gain_grad), "gy", "gx"
     )
     shrink = clip_factor(
         jnp.sum(combined * combined) + jnp.sum(gain_summed * gain_summed), channels

time: 334 us -> 354 us (1.060)
  waiting for transfers between devices: 128 us -> 165 us
  blocking collectives: 45 us -> 28.7 us
    psum x1 -> x2, waiting for transfers between devices: 124 us -> 161 us  [the longest x1 90.5 us: axis_by_axis(): return lax.psum(inner, outer_axis)]
    psum x1 -> x2, blocking collectives: 45 us -> 28.7 us  [the longest x1 17.7 us: axis_by_axis(): inner = lax.psum(value, inner_axis)]
    unnamed x328 -> x334, local copies, waits for them, and re-layouts: 10.5 us -> 9.86 us
  transfers between devices with their start and end apart: 17 -> 18, of which waited for: 3 -> 4; matrix products, arithmetic and copies ran while one was open for 9% -> 9% of each run, Pallas kernels for 0% -> 0%
where the time goes in v1:
time: 354 us; the launch traced here: 352 us
  waiting for transfers between devices  165 us (47%)
  matrix products  44.1 us (12%)
  starting transfers between devices  36 us (10%)
  local copies, waits for them, and re-layouts  35.6 us (10%)
  blocking collectives  28.7 us (8%)
  other arithmetic  23.9 us (7%)
  between operations  18.7 us (5%)
    psum x1, waiting for transfers between devices, axis_by_axis(): return lax.psum(inner, outer_axis)  90.5 us
    psum x1, waiting for transfers between devices, axis_by_axis(): inner = lax.psum(value, inner_axis)  70.4 us
    ppermute x8, starting transfers between devices, with_halo(): lax.ppermute(tail, axis, [(i, (i + 1) % count) for i in range(ends)])  25.2 us
    psum x1, blocking collectives, axis_by_axis(): inner = lax.psum(value, inner_axis)  17.7 us
    dot_general x54, matrix products, tap_grads(): lax.dot_general(window, flat_rows, (((0,), (0,)), ((), ())), preferred_el...  15.4 us
    dot_general x54, matrix products, apply_taps(): jnp.dot(window, kernel[tap_index], preferred_element_type=jnp.float32)  14.4 us
    dot_general x54, matrix products, apply_taps(): lax.dot_general(window, kernel[tap_index], (((1,), (1,)), ((), ())), pref...  14.3 us
    slice x8, local copies, waits for them, and re-layouts, apply_taps(): tile_set[:, start_x:start_x + 8, start_y:start_y + 8, start_z:start_z + 8...  13.7 us
  transfers between devices with their start and end apart: 18, of which 4 were waited for; matrix products, arithmetic and copies ran while one was open for 9% of the time, Pallas kernels for 0%

profile of v1, /device:TPU:0, one launch (start us, length us, event | category | flops | bytes accessed | tf_op | source)
XLA Modules:
  0.0 352.0 jit_solution(16772888888324633538)
XLA Ops:
  9.2 1.1 broadcast_select_fusion
  11.2 4.9 %collective-permute-start.8 = (bf16[1,16,8,128]{3,2,1,0:T(8,128)(2,1)S(1)}, bf16[1,16,8,128]{3,2,1,0:T(8,128)(2,1)S(1)}, u32[]{:S(2)}, u32[]{:S(2)}) collective-permute-start(bf16[1,16,8,128]{3,2,1,0:T(8,128)(2,1)S(1)} %get-tuple-element.24), channel_id=1, source_target_pairs={{0,8},{8,16},{16,24},{1,9},{9,17},{17,25},{2,10},{10,18},{18,26},{... | collective-permute-start | bytes 98312 | tf_op jit(solution)/shard_map/ppermute | solution.py:26
  16.1 1.3 collective-permute-start.9
  18.3 4.5 %collective-permute-start = (bf16[1,16,8,128]{3,2,1,0:T(8,128)(2,1)S(1)}, bf16[1,16,8,128]{3,2,1,0:T(8,128)(2,1)S(1)}, u32[]{:S(2)}, u32[]{:S(2)}) collective-permute-start(bf16[1,16,8,128]{3,2,1,0:T(8,128)(2,1)S(1)} %get-tuple-element.28), channel_id=1, source_target_pairs={{0,8},{8,16},{16,24},{1,9},{9,17},{17,25},{2,10},{10,18},{18,26},{... | collective-permute-start | bytes 98312 | tf_op jit(solution)/shard_map/ppermute | solution.py:26
  22.8 1.3 collective-permute-start.1
  24.3 1.3 collective-permute-start.10
  25.6 1.3 collective-permute-start.11
  26.9 2.1 collective-permute-done.1
  29.0 2.7 collective-permute-start.2
  31.8 1.3 collective-permute-start.3
  33.9 2.8 pad_slice_fusion.18
  36.6 1.4 fusion.300
  39.2 1.2 pad_slice_fusion.54
  56.2 2.5 multiply_reduce_fusion.1
  59.4 2.9 fusion.293
  62.5 1.5 select_convert_fusion
  64.3 1.3 fusion.52
  72.9 1.2 copy-done.94
  74.2 1.7 fusion.62
  76.8 4.9 %collective-permute-start.4 = (bf16[1,16,8,128]{3,2,1,0:T(8,128)(2,1)S(1)}, bf16[1,16,8,128]{3,2,1,0:T(8,128)(2,1)S(1)}, u32[]{:S(2)}, u32[]{:S(2)}) collective-permute-start(bf16[1,16,8,128]{3,2,1,0:T(8,128)(2,1)S(1)} %get-tuple-element.26), channel_id=1, source_target_pairs={{0,8},{8,16},{16,24},{1,9},{9,17},{17,25},{2,10},{10,18},{18,26},{... | collective-permute-start | bytes 98312 | tf_op jit(solution)/shard_map/ppermute | solution.py:26
  81.7 1.3 collective-permute-start.5
  83.1 17.7 %psum.30 = f32[128]{0:T(128)S(1)} all-reduce(f32[128]{0:T(128)S(1)} %copy-done.166), channel_id=1, replica_groups=mesh['gx'=4,'gy'=8] {'gy'}, use_global_device_ids=true, to_apply=%region_12.13 | all-reduce | flops 128 | bytes 1024 | tf_op jit(solution)/shard_map/psum | solution.py:14
  100.7 11.0 %psum.31 = f32[128]{0:T(128)S(1)} all-reduce(f32[128]{0:T(128)S(1)} %psum.30), channel_id=1, replica_groups=mesh['gx'=4,'gy'=8] {'gx'}, use_global_device_ids=true, to_apply=%region_13.14 | all-reduce | flops 128 | bytes 1024 | tf_op jit(solution)/shard_map/psum | solution.py:15
  112.7 2.2 scatter_fusion.3
  114.9 1.1 copy.13
  116.6 3.6 %collective-permute-start.12 = (bf16[1,16,8,128]{3,2,1,0:T(8,128)(2,1)S(1)}, bf16[1,16,8,128]{3,2,1,0:T(8,128)(2,1)S(1)}, u32[]{:S(2)}, u32[]{:S(2)}) collective-permute-start(bf16[1,16,8,128]{3,2,1,0:T(8,128)(2,1)S(1)} %get-tuple-element.22), channel_id=1, source_target_pairs={{0,8},{8,16},{16,24},{1,9},{9,17},{17,25},{2,10},{10,18},{18,26},{... | collective-permute-start | bytes 98312 | tf_op jit(solution)/shard_map/ppermute | solution.py:26
  120.2 1.3 collective-permute-start.13
  121.6 1.3 collective-permute-start.6
  122.9 1.3 collective-permute-start.7
  124.2 1.8 collective-permute-done.13
  126.7 1.9 collective-permute-start.14
  128.6 1.5 collective-permute-start.15
  131.1 1.8 gather_fusion.1
  132.9 2.6 pad_slice_fusion.36
  135.5 1.3 fusion.301
  136.9 1.8 pad_maximum_fusion.4
  138.6 1.8 gather_fusion.3
  140.5 2.7 pad_slice_fusion
  143.2 1.4 fusion.299
  144.6 1.0 fusion.117
  153.5 2.0 pad_maximum_fusion
  155.9 1.4 convolution_add_fusion.77
  157.3 1.2 convolution_add_fusion.76
  170.5 70.4 %all-reduce.7.cloned.1.call-done = f32[884736]{0:T(1024)} async-done(((f32[884736]{0:T(1024)}), f32[884736]{0:T(1024)}) %all-reduce.7.cloned.1.call-update) | async-done | bytes 3538960 | tf_op jit(solution)/shard_map/psum | solution.py:14
  246.1 1.0 select_convert_fusion.1
  247.1 90.5 %all-reduce.9.cloned.1.call-done = f32[884736]{0:T(1024)} async-done(((f32[884736]{0:T(1024)}), f32[884736]{0:T(1024)}) %all-reduce.9.cloned.1.call-update) | async-done | bytes 3538960 | tf_op jit(solution)/shard_map/psum | solution.py:15
  337.6 3.7 %multiply_reduce_fusion = f32[]{:T(128)} fusion(f32[884736]{0:T(1024)} %all-reduce.9.cloned.1.call-done), kind=kLoop, calls=%fused_computation.9 | loop fusion | flops 1769471 | bytes 3538948 | tf_op jit(solution)/shard_map/reduce_sum | solution.py:155
  343.1 2.0 broadcast_multiply_fusion
  (549 shorter events, 57.5 us)
Async XLA Ops:
  7.2 233.7 %all-reduce.7.cloned.1.call-start = ((), (), s32[]{:S(2)}) async-start(), calls=%async_computation | async-start | bytes 7077888 | tf_op jit(solution)/shard_map/psum | solution.py:14
  7.9 30.3 %copy-start.152 = (s32[2]{0:T(128)}, s32[2]{0:T(128)S(1)}, u32[]{:S(2)}) copy-start(s32[2]{0:T(128)S(1)} %get-tuple-element.9) | copy-start | bytes 28
  8.6 15.6 %copy-start.159 = (pred[2]{0:T(512)(128)(4,1)}, pred[2]{0:T(512)(128)(4,1)S(1)}, u32[]{:S(2)}) copy-start(pred[2]{0:T(512)(128)(4,1)S(1)} %broadcast_compare_fusion) | copy-start | bytes 10
  9.2 8.3 %copy-start.153 = (s32[2]{0:T(128)}, s32[2]{0:T(128)S(1)}, u32[]{:S(2)}) copy-start(s32[2]{0:T(128)S(1)} %fusion.291) | copy-start | bytes 28
  11.2 13.0 %collective-permute-start.8 = (bf16[1,16,8,128]{3,2,1,0:T(8,128)(2,1)S(1)}, bf16[1,16,8,128]{3,2,1,0:T(8,128)(2,1)S(1)}, u32[]{:S(2)}, u32[]{:S(2)}) collective-permute-start(bf16[1,16,8,128]{3,2,1,0:T(8,128)(2,1)S(1)} %get-tuple-element.24), channel_id=1, source_target_pairs={{0,8},{8,16},{16,24},{1,9},{9,17},{17,25},{2,10},{10,18},{18,26},{... | collective-permute-start | bytes 98312 | tf_op jit(solution)/shard_map/ppermute | solution.py:26
  16.1 8.1 %collective-permute-start.9 = (bf16[1,16,8,128]{3,2,1,0:T(8,128)(2,1)S(1)}, bf16[1,16,8,128]{3,2,1,0:T(8,128)(2,1)S(1)}, u32[]{:S(2)}, u32[]{:S(2)}) collective-permute-start(bf16[1,16,8,128]{3,2,1,0:T(8,128)(2,1)S(1)} %get-tuple-element.25), channel_id=1, source_target_pairs={{8,0},{16,8},{24,16},{9,1},{17,9},{25,17},{10,2},{18,10},{26,18},{... | collective-permute-start | bytes 98312 | tf_op jit(solution)/shard_map/ppermute | solution.py:28
  18.3 8.6 %collective-permute-start = (bf16[1,16,8,128]{3,2,1,0:T(8,128)(2,1)S(1)}, bf16[1,16,8,128]{3,2,1,0:T(8,128)(2,1)S(1)}, u32[]{:S(2)}, u32[]{:S(2)}) collective-permute-start(bf16[1,16,8,128]{3,2,1,0:T(8,128)(2,1)S(1)} %get-tuple-element.28), channel_id=1, source_target_pairs={{0,8},{8,16},{16,24},{1,9},{9,17},{17,25},{2,10},{10,18},{18,26},{... | collective-permute-start | bytes 98312 | tf_op jit(solution)/shard_map/ppermute | solution.py:26
  22.8 6.2 %collective-permute-start.1 = (bf16[1,16,8,128]{3,2,1,0:T(8,128)(2,1)S(1)}, bf16[1,16,8,128]{3,2,1,0:T(8,128)(2,1)S(1)}, u32[]{:S(2)}, u32[]{:S(2)}) collective-permute-start(bf16[1,16,8,128]{3,2,1,0:T(8,128)(2,1)S(1)} %get-tuple-element.29), channel_id=1, source_target_pairs={{8,0},{16,8},{24,16},{9,1},{17,9},{25,17},{10,2},{18,10},{26,18},{... | collective-permute-start | bytes 98312 | tf_op jit(solution)/shard_map/ppermute | solution.py:28
  24.2 31.9 %copy-start.156 = (pred[1024]{0:T(1024)(128)(4,1)}, pred[1024]{0:T(1024)(128)(4,1)S(1)}, u32[]{:S(2)}) copy-start(pred[1024]{0:T(1024)(128)(4,1)S(1)} %broadcast_in_dim.109) | copy-start | bytes 3076
  24.3 8.8 %collective-permute-start.10 = (bf16[18,1,8,128]{3,2,1,0:T(8,128)(2,1)S(1)}, bf16[18,1,8,128]{3,2,1,0:T(8,128)(2,1)S(1)}, u32[]{:S(2)}, u32[]{:S(2)}) collective-permute-start(bf16[18,1,8,128]{3,2,1,0:T(8,128)(2,1)S(1)} %get-tuple-element.16), channel_id=1, source_target_pairs={{0,1},{1,2},{2,3},{3,4},{4,5},{5,6},{6,7},{8,9},{9,10},{10,11},{11... | collective-permute-start | bytes 110600 | tf_op jit(solution)/shard_map/ppermute | solution.py:26
  25.6 7.5 %collective-permute-start.11 = (bf16[18,1,8,128]{3,2,1,0:T(8,128)(2,1)S(1)}, bf16[18,1,8,128]{3,2,1,0:T(8,128)(2,1)S(1)}, u32[]{:S(2)}, u32[]{:S(2)}) collective-permute-start(bf16[18,1,8,128]{3,2,1,0:T(8,128)(2,1)S(1)} %get-tuple-element.17), channel_id=1, source_target_pairs={{1,0},{2,1},{3,2},{4,3},{5,4},{6,5},{7,6},{9,8},{10,9},{11,10},{12... | collective-permute-start | bytes 110600 | tf_op jit(solution)/shard_map/ppermute | solution.py:28
  29.0 9.0 %collective-permute-start.2 = (bf16[18,1,8,128]{3,2,1,0:T(8,128)(2,1)S(1)}, bf16[18,1,8,128]{3,2,1,0:T(8,128)(2,1)S(1)}, u32[]{:S(2)}, u32[]{:S(2)}) collective-permute-start(bf16[18,1,8,128]{3,2,1,0:T(8,128)(2,1)S(1)} %get-tuple-element.20), channel_id=1, source_target_pairs={{0,1},{1,2},{2,3},{3,4},{4,5},{5,6},{6,7},{8,9},{9,10},{10,11},{11... | collective-permute-start | bytes 110600 | tf_op jit(solution)/shard_map/ppermute | solution.py:26
  31.8 6.3 %collective-permute-start.3 = (bf16[18,1,8,128]{3,2,1,0:T(8,128)(2,1)S(1)}, bf16[18,1,8,128]{3,2,1,0:T(8,128)(2,1)S(1)}, u32[]{:S(2)}, u32[]{:S(2)}) collective-permute-start(bf16[18,1,8,128]{3,2,1,0:T(8,128)(2,1)S(1)} %get-tuple-element.21), channel_id=1, source_target_pairs={{1,0},{2,1},{3,2},{4,3},{5,4},{6,5},{7,6},{9,8},{10,9},{11,10},{12... | collective-permute-start | bytes 110600 | tf_op jit(solution)/shard_map/ppermute | solution.py:28
  39.2 3.3 copy-start.31
  39.2 4.0 %copy-start.25 = (bf16[2,8,8,8,128]{4,3,2,1,0:T(8,128)(2,1)}, bf16[2,8,8,8,128]{4,3,2,1,0:T(8,128)(2,1)S(1)}, u32[]{:S(2)}) copy-start(bf16[2,8,8,8,128]{4,3,2,1,0:T(8,128)(2,1)S(1)} %get-tuple-element.133) | copy-start | bytes 786436
  39.2 4.6 %copy-start.17 = (bf16[2,8,8,8,128]{4,3,2,1,0:T(8,128)(2,1)}, bf16[2,8,8,8,128]{4,3,2,1,0:T(8,128)(2,1)S(1)}, u32[]{:S(2)}) copy-start(bf16[2,8,8,8,128]{4,3,2,1,0:T(8,128)(2,1)S(1)} %get-tuple-element.132) | copy-start | bytes 786436
  39.2 5.3 %copy-start.7 = (bf16[2,8,8,8,128]{4,3,2,1,0:T(8,128)(2,1)}, bf16[2,8,8,8,128]{4,3,2,1,0:T(8,128)(2,1)S(1)}, u32[]{:S(2)}) copy-start(bf16[2,8,8,8,128]{4,3,2,1,0:T(8,128)(2,1)S(1)} %get-tuple-element.131) | copy-start | bytes 786436
  40.5 3.1 copy-start.29
  40.5 3.5 %copy-start.27 = (bf16[2,8,8,8,128]{4,3,2,1,0:T(8,128)(2,1)}, bf16[2,8,8,8,128]{4,3,2,1,0:T(8,128)(2,1)S(1)}, u32[]{:S(2)}) copy-start(bf16[2,8,8,8,128]{4,3,2,1,0:T(8,128)(2,1)S(1)} %get-tuple-element.120) | copy-start | bytes 786436
  40.6 3.8 %copy-start.23 = (bf16[2,8,8,8,128]{4,3,2,1,0:T(8,128)(2,1)}, bf16[2,8,8,8,128]{4,3,2,1,0:T(8,128)(2,1)S(1)}, u32[]{:S(2)}) copy-start(bf16[2,8,8,8,128]{4,3,2,1,0:T(8,128)(2,1)S(1)} %get-tuple-element.121) | copy-start | bytes 786436
  40.6 4.2 %copy-start.21 = (bf16[2,8,8,8,128]{4,3,2,1,0:T(8,128)(2,1)}, bf16[2,8,8,8,128]{4,3,2,1,0:T(8,128)(2,1)S(1)}, u32[]{:S(2)}) copy-start(bf16[2,8,8,8,128]{4,3,2,1,0:T(8,128)(2,1)S(1)} %get-tuple-element.122) | copy-start | bytes 786436
  40.6 4.4 %copy-start.19 = (bf16[2,8,8,8,128]{4,3,2,1,0:T(8,128)(2,1)}, bf16[2,8,8,8,128]{4,3,2,1,0:T(8,128)(2,1)S(1)}, u32[]{:S(2)}) copy-start(bf16[2,8,8,8,128]{4,3,2,1,0:T(8,128)(2,1)S(1)} %get-tuple-element.123) | copy-start | bytes 786436
  40.6 4.6 %copy-start.15 = (bf16[2,8,8,8,128]{4,3,2,1,0:T(8,128)(2,1)}, bf16[2,8,8,8,128]{4,3,2,1,0:T(8,128)(2,1)S(1)}, u32[]{:S(2)}) copy-start(bf16[2,8,8,8,128]{4,3,2,1,0:T(8,128)(2,1)S(1)} %get-tuple-element.129) | copy-start | bytes 786436
  40.6 4.8 %copy-start.13 = (bf16[2,8,8,8,128]{4,3,2,1,0:T(8,128)(2,1)}, bf16[2,8,8,8,128]{4,3,2,1,0:T(8,128)(2,1)S(1)}, u32[]{:S(2)}) copy-start(bf16[2,8,8,8,128]{4,3,2,1,0:T(8,128)(2,1)S(1)} %get-tuple-element.124) | copy-start | bytes 786436
  40.6 5.1 %copy-start.11 = (bf16[2,8,8,8,128]{4,3,2,1,0:T(8,128)(2,1)}, bf16[2,8,8,8,128]{4,3,2,1,0:T(8,128)(2,1)S(1)}, u32[]{:S(2)}) copy-start(bf16[2,8,8,8,128]{4,3,2,1,0:T(8,128)(2,1)S(1)} %get-tuple-element.125) | copy-start | bytes 786436
  40.6 5.3 %copy-start.9 = (bf16[2,8,8,8,128]{4,3,2,1,0:T(8,128)(2,1)}, bf16[2,8,8,8,128]{4,3,2,1,0:T(8,128)(2,1)S(1)}, u32[]{:S(2)}) copy-start(bf16[2,8,8,8,128]{4,3,2,1,0:T(8,128)(2,1)S(1)} %get-tuple-element.128) | copy-start | bytes 786436
  40.6 5.5 %copy-start.5 = (bf16[2,8,8,8,128]{4,3,2,1,0:T(8,128)(2,1)}, bf16[2,8,8,8,128]{4,3,2,1,0:T(8,128)(2,1)S(1)}, u32[]{:S(2)}) copy-start(bf16[2,8,8,8,128]{4,3,2,1,0:T(8,128)(2,1)S(1)} %get-tuple-element.126) | copy-start | bytes 786436
  40.6 5.7 %copy-start.3 = (bf16[2,8,8,8,128]{4,3,2,1,0:T(8,128)(2,1)}, bf16[2,8,8,8,128]{4,3,2,1,0:T(8,128)(2,1)S(1)}, u32[]{:S(2)}) copy-start(bf16[2,8,8,8,128]{4,3,2,1,0:T(8,128)(2,1)S(1)} %get-tuple-element.127) | copy-start | bytes 786436
  58.7 3.8 %copy-start.157 = (pred[1024]{0:T(1024)(128)(4,1)S(1)}, pred[1024]{0:T(1024)(128)(4,1)}, u32[]{:S(2)}) copy-start(pred[1024]{0:T(1024)(128)(4,1)} %copy-done.156) | copy-start | bytes 3076
  62.4 3.1 copy-start.51
  62.4 3.4 copy-start.48
  62.5 3.7 %copy-start.40 = (bf16[2,8,8,8,128]{4,3,2,1,0:T(8,128)(2,1)S(1)}, bf16[2,8,8,8,128]{4,3,2,1,0:T(8,128)(2,1)}, u32[]{:S(2)}) copy-start(bf16[2,8,8,8,128]{4,3,2,1,0:T(8,128)(2,1)} %copy-done.39) | copy-start | bytes 786436
  62.5 3.9 %copy-start.44 = (bf16[2,8,8,8,128]{4,3,2,1,0:T(8,128)(2,1)S(1)}, bf16[2,8,8,8,128]{4,3,2,1,0:T(8,128)(2,1)}, u32[]{:S(2)}) copy-start(bf16[2,8,8,8,128]{4,3,2,1,0:T(8,128)(2,1)} %copy-done.43) | copy-start | bytes 786436
  72.6 3.5 copy-start.154
  74.2 8.8 %copy-start.166 = (f32[128]{0:T(128)S(1)}, f32[128]{0:T(128)}, u32[]{:S(2)}) copy-start(f32[128]{0:T(128)} %get-tuple-element.4) | copy-start | bytes 1540
  75.9 36.7 %copy-start.155 = (s32[2]{0:T(128)S(1)}, s32[2]{0:T(128)}, u32[]{:S(2)}) copy-start(s32[2]{0:T(128)} %copy-done.153) | copy-start | bytes 28
  76.8 44.7 %collective-permute-start.4 = (bf16[1,16,8,128]{3,2,1,0:T(8,128)(2,1)S(1)}, bf16[1,16,8,128]{3,2,1,0:T(8,128)(2,1)S(1)}, u32[]{:S(2)}, u32[]{:S(2)}) collective-permute-start(bf16[1,16,8,128]{3,2,1,0:T(8,128)(2,1)S(1)} %get-tuple-element.26), channel_id=1, source_target_pairs={{0,8},{8,16},{16,24},{1,9},{9,17},{17,25},{2,10},{10,18},{18,26},{... | collective-permute-start | bytes 98312 | tf_op jit(solution)/shard_map/ppermute | solution.py:26
  81.7 39.8 %collective-permute-start.5 = (bf16[1,16,8,128]{3,2,1,0:T(8,128)(2,1)S(1)}, bf16[1,16,8,128]{3,2,1,0:T(8,128)(2,1)S(1)}, u32[]{:S(2)}, u32[]{:S(2)}) collective-permute-start(bf16[1,16,8,128]{3,2,1,0:T(8,128)(2,1)S(1)} %get-tuple-element.27), channel_id=1, source_target_pairs={{8,0},{16,8},{24,16},{9,1},{17,9},{25,17},{10,2},{18,10},{26,18},{... | collective-permute-start | bytes 98312 | tf_op jit(solution)/shard_map/ppermute | solution.py:28
  111.7 9.8 %copy-start.164 = (f32[128]{0:T(128)}, f32[128]{0:T(128)S(1)}, u32[]{:S(2)}) copy-start(f32[128]{0:T(128)S(1)} %psum.31) | copy-start | bytes 1540
  116.6 7.6 %collective-permute-start.12 = (bf16[1,16,8,128]{3,2,1,0:T(8,128)(2,1)S(1)}, bf16[1,16,8,128]{3,2,1,0:T(8,128)(2,1)S(1)}, u32[]{:S(2)}, u32[]{:S(2)}) collective-permute-start(bf16[1,16,8,128]{3,2,1,0:T(8,128)(2,1)S(1)} %get-tuple-element.22), channel_id=1, source_target_pairs={{0,8},{8,16},{16,24},{1,9},{9,17},{17,25},{2,10},{10,18},{18,26},{... | collective-permute-start | bytes 98312 | tf_op jit(solution)/shard_map/ppermute | solution.py:26
  120.2 5.8 %collective-permute-start.13 = (bf16[1,16,8,128]{3,2,1,0:T(8,128)(2,1)S(1)}, bf16[1,16,8,128]{3,2,1,0:T(8,128)(2,1)S(1)}, u32[]{:S(2)}, u32[]{:S(2)}) collective-permute-start(bf16[1,16,8,128]{3,2,1,0:T(8,128)(2,1)S(1)} %get-tuple-element.23), channel_id=1, source_target_pairs={{8,0},{16,8},{24,16},{9,1},{17,9},{25,17},{10,2},{18,10},{26,18},{... | collective-permute-start | bytes 98312 | tf_op jit(solution)/shard_map/ppermute | solution.py:28
  121.6 8.5 %collective-permute-start.6 = (bf16[18,1,8,128]{3,2,1,0:T(8,128)(2,1)S(1)}, bf16[18,1,8,128]{3,2,1,0:T(8,128)(2,1)S(1)}, u32[]{:S(2)}, u32[]{:S(2)}) collective-permute-start(bf16[18,1,8,128]{3,2,1,0:T(8,128)(2,1)S(1)} %get-tuple-element.18), channel_id=1, source_target_pairs={{0,1},{1,2},{2,3},{3,4},{4,5},{5,6},{6,7},{8,9},{9,10},{10,11},{11... | collective-permute-start | bytes 110600 | tf_op jit(solution)/shard_map/ppermute | solution.py:26
  122.9 7.2 %collective-permute-start.7 = (bf16[18,1,8,128]{3,2,1,0:T(8,128)(2,1)S(1)}, bf16[18,1,8,128]{3,2,1,0:T(8,128)(2,1)S(1)}, u32[]{:S(2)}, u32[]{:S(2)}) collective-permute-start(bf16[18,1,8,128]{3,2,1,0:T(8,128)(2,1)S(1)} %get-tuple-element.19), channel_id=1, source_target_pairs={{1,0},{2,1},{3,2},{4,3},{5,4},{6,5},{7,6},{9,8},{10,9},{11,10},{12... | collective-permute-start | bytes 110600 | tf_op jit(solution)/shard_map/ppermute | solution.py:28
  126.7 10.2 %collective-permute-start.14 = (bf16[18,1,8,128]{3,2,1,0:T(8,128)(2,1)}, bf16[18,1,8,128]{3,2,1,0:T(8,128)(2,1)}, u32[]{:S(2)}, u32[]{:S(2)}) collective-permute-start(bf16[18,1,8,128]{3,2,1,0:T(8,128)(2,1)} %get-tuple-element.14), channel_id=1, source_target_pairs={{0,1},{1,2},{2,3},{3,4},{4,5},{5,6},{6,7},{8,9},{9,10},{10,11},{11... | collective-permute-start | bytes 110600 | tf_op jit(solution)/shard_map/ppermute | solution.py:26
  128.6 8.3 %collective-permute-start.15 = (bf16[18,1,8,128]{3,2,1,0:T(8,128)(2,1)}, bf16[18,1,8,128]{3,2,1,0:T(8,128)(2,1)}, u32[]{:S(2)}, u32[]{:S(2)}) collective-permute-start(bf16[18,1,8,128]{3,2,1,0:T(8,128)(2,1)} %get-tuple-element.15), channel_id=1, source_target_pairs={{1,0},{2,1},{3,2},{4,3},{5,4},{6,5},{7,6},{9,8},{10,9},{11,10},{12... | collective-permute-start | bytes 110600 | tf_op jit(solution)/shard_map/ppermute | solution.py:28
  155.6 182.0 %all-reduce.9.cloned.1.call-start = ((), (), s32[]{:S(2)}) async-start(), calls=%async_computation.1 | async-start | bytes 7077888 | tf_op jit(solution)/shard_map/psum | solution.py:15
  247.1 95.5 %copy-start.165 = (f32[128]{0:T(128)S(1)}, f32[128]{0:T(128)}, u32[]{:S(2)}) copy-start(f32[128]{0:T(128)} %copy-done.164) | copy-start | bytes 1540
  337.6 5.5 %copy-start = (f32[884736]{0:T(1024)S(1)}, f32[884736]{0:T(1024)}, u32[]{:S(2)}) copy-start(f32[884736]{0:T(1024)} %all-reduce.9.cloned.1.call-done) | copy-start | bytes 10616836
  (137 other events, 197.0 us)
Sparse Core Ops, SparseCore 0:
  155.7 85.1 all-reduce.6
  244.0 93.5 all-reduce.8
